TPU v7x, 256 devices: a whole 4x4x8 slice. The times are simulated.
256 devices in a mesh: dp: 8 (over z_lo, x), seq: 32 (over y, z_hi, core).
Axes of the slice: x: 4, y: 4, z: 8 (z_hi: 4, z_lo: 2; z = z_hi * 2 + z_lo), core: 2. Of those that a mesh axis runs over, the one named last changes fastest.
Arguments:
- queries: bfloat16 [8, 4096, 4096], P('dp', 'seq'), may hold values from -5 to 5
- rotated_key_rows: bfloat16 [8, 4096, 512], P('dp', 'seq'), may hold values from -5 to 5
- hidden_states: bfloat16 [8, 4096, 8192], P('dp', 'seq'), may hold values from -6 to 6
- block_order: int32 [64], replicated, may hold values from 0 to 63, each once
- first_weight: bfloat16 [8192, 512], replicated, may hold values from -0.0625 to 0.0625
- first_bias: float32 [512], replicated, may hold values from -3 to 3
- output_weight: bfloat16 [4, 512], replicated, may hold values from -0.25 to 0.25
- output_bias: float32 [4], replicated, may hold values from -1 to 1
Outputs:
- token_attention_mass: float32 [8, 4, 4096], P('dp', None, 'seq')
- loss_value: float32 [], replicated
- step_first: float32 [8192, 512], P('seq')
- output_weight_step: float32 [4, 512], replicated
- step_bias: float32 [512], replicated
- grad_bias: float32 [4], replicated
All inputs are finite; a program needn't handle non-finite values.
Results may differ from a plain program's by a relative error of at most 0.0023.
Values may be sent and summed in bfloat16 or wider, within the bound.
A program may use at most 64 MiB of HBM per device.

v0:
```python
import math
import jax
import jax.numpy as jnp
from jax import lax
from jax.sharding import PartitionSpec as P

D = 8192
KEY_VALUE_HEADS = 4
HEAD_SIZE = 128
RETAIN_HIDDEN = 512
BLK = 64
QUERY_GROUP_SIZE = 8


def key_places(block_order, offset, amount):
    row_ids = offset + lax.iota(jnp.int32, amount)
    block_ids = row_ids // BLK
    block_table = lax.iota(jnp.int32, block_order.shape[0])
    anchor = jnp.sum(
        jnp.where(block_ids[:, None] == block_table[None, :], block_order[None, :], 0), axis=1
    )
    return anchor * BLK + row_ids % BLK


def raw_scores(head_queries, mass_portion):
    head_keys = mass_portion.reshape(mass_portion.shape[0], KEY_VALUE_HEADS, HEAD_SIZE)
    return jnp.einsum(
        "tkgd,nkd->kgtn", head_queries, head_keys, preferred_element_type=jnp.float32
    ) * HEAD_SIZE ** (-0.5)


def blockwise(mass_portion, offset, update, carried):
    rows_here = mass_portion.shape[0]
    inner = math.gcd(rows_here, BLK)

    def visit_block(step_index, running):
        local_start = step_index * inner
        sub_rows = lax.dynamic_slice_in_dim(mass_portion, local_start, inner, 0)
        return update(running, sub_rows, offset + local_start)

    return lax.fori_loop(0, rows_here // inner, visit_block, carried)


def normalizer_step(running, mass_portion, key_start, head_queries, query_pos, block_order):
    highest, summed = running
    key_pos = key_places(block_order, key_start, mass_portion.shape[0])

    def normalizer_compute_step():
        scores = raw_scores(head_queries, mass_portion)
        visible = query_pos[:, None] >= key_pos[None, :]
        masked = jnp.where(visible, scores, -1e30)
        raised = jnp.maximum(highest, jnp.max(masked, axis=-1))
        exponents = jnp.where(visible, jnp.exp(masked - raised[..., None]), 0.0)
        return (raised, summed * jnp.exp(highest - raised) + jnp.sum(exponents, axis=-1))

    return lax.cond(
        jnp.min(key_pos) > jnp.max(query_pos), lambda: (highest, summed), normalizer_compute_step
    )


def mass_step(mass_portion, key_start, head_queries, query_pos, log_total, block_order):
    amount = mass_portion.shape[0]
    key_pos = key_places(block_order, key_start, amount)

    def mass_compute_step():
        scores = raw_scores(head_queries, mass_portion)
        visible = query_pos[:, None] >= key_pos[None, :]
        masked = jnp.where(visible, scores, -1e30)
        weights = jnp.where(visible, jnp.exp(masked - log_total[..., None]), 0.0)
        return jnp.sum(weights, axis=(1, 2)) / QUERY_GROUP_SIZE

    return lax.cond(
        jnp.min(key_pos) > jnp.max(query_pos),
        lambda: jnp.zeros((KEY_VALUE_HEADS, amount), jnp.float32),
        mass_compute_step,
    )


def normalized_scores(value_rows, square_sum, entries):
    return value_rows / jnp.sqrt(square_sum / entries + 1e-06)


def per_device(
    queries,
    rotated_key_rows,
    hidden_states,
    block_order,
    first_weight,
    first_bias,
    output_weight,
    output_bias,
):
    local_row_slice = queries.shape[1]
    total_length = local_row_slice * lax.axis_size("seq")
    head_queries = queries.reshape(local_row_slice, KEY_VALUE_HEADS, QUERY_GROUP_SIZE, HEAD_SIZE)
    local_key_rows = rotated_key_rows.reshape(local_row_slice, KEY_VALUE_HEADS * HEAD_SIZE)
    query_pos = key_places(block_order, lax.axis_index("seq") * local_row_slice, local_row_slice)
    start_state = (
        jnp.full((KEY_VALUE_HEADS, QUERY_GROUP_SIZE, local_row_slice), -1e30, jnp.float32),
        jnp.zeros((KEY_VALUE_HEADS, QUERY_GROUP_SIZE, local_row_slice), jnp.float32),
    )

    def norm_update(running, sub_rows, key_start):
        return normalizer_step(running, sub_rows, key_start, head_queries, query_pos, block_order)

    empty_mass = jnp.zeros((KEY_VALUE_HEADS, total_length), jnp.float32)
    keys_whole = lax.all_gather(local_key_rows, "seq", axis=0, tiled=True)
    highest, summed = blockwise(keys_whole, 0, norm_update, start_state)
    log_total = highest + jnp.log(summed)

    def add_kept(collected, sub_rows, key_start):
        term = mass_step(sub_rows, key_start, head_queries, query_pos, log_total, block_order)
        return lax.dynamic_update_slice_in_dim(collected, term, key_start, 1)

    column_mass = blockwise(keys_whole, 0, add_kept, empty_mass)
    key_attention_mass = lax.psum_scatter(column_mass, "seq", scatter_dimension=1, tiled=True)
    tokens_in = hidden_states.reshape(local_row_slice, hidden_states.shape[2])
    pre_act = jnp.dot(tokens_in, first_weight, preferred_element_type=jnp.float32) + first_bias
    hidden = jax.nn.silu(pre_act).astype(jnp.bfloat16)
    predicted_scores = (
        lax.dot_general(
            output_weight, hidden, (((1,), (1,)), ((), ())), preferred_element_type=jnp.float32
        )
        + output_bias[:, None]
    )
    score_residue = predicted_scores - jnp.log(1.0 + key_attention_mass)
    loss_part = 0.5 * jnp.sum(score_residue * score_residue) / total_length
    out_grad = score_residue / total_length
    bias_part = jnp.sum(out_grad, axis=1)
    second_part = jnp.dot(out_grad, hidden.astype(jnp.float32), precision=lax.Precision.HIGHEST)
    back_grad = jnp.dot(
        out_grad.T, output_weight.astype(jnp.float32), precision=lax.Precision.HIGHEST
    )
    gate_value = jax.nn.sigmoid(pre_act)
    slope_grad = back_grad * gate_value * (1.0 + pre_act * (1.0 - gate_value))
    first_bias_part = jnp.sum(slope_grad, axis=0)
    slope_half = slope_grad.astype(jnp.bfloat16)
    columns_all = lax.all_to_all(tokens_in, "seq", split_axis=1, concat_axis=0, tiled=True)
    slope_all = lax.all_gather(slope_half, "seq", axis=0, tiled=True)
    first_shard = lax.dot_general(
        columns_all, slope_all, (((0,), (0,)), ((), ())), preferred_element_type=jnp.float32
    )
    output_total, first_bias_total, bias_total, loss_total = lax.psum(
        (second_part, first_bias_part, bias_part, loss_part), ("dp", "seq")
    )
    first_grad = lax.psum(first_shard, "dp")
    first_square = lax.psum(jnp.sum(first_grad * first_grad), "seq")
    step_first = normalized_scores(first_grad, first_square, D * RETAIN_HIDDEN)
    output_weight_step = normalized_scores(
        output_total, jnp.sum(output_total * output_total), RETAIN_HIDDEN * KEY_VALUE_HEADS
    )
    step_bias = normalized_scores(
        first_bias_total, jnp.sum(first_bias_total * first_bias_total), RETAIN_HIDDEN
    )
    return (
        key_attention_mass.reshape(1, KEY_VALUE_HEADS, local_row_slice),
        loss_total,
        step_first,
        output_weight_step,
        step_bias,
        bias_total,
    )


def solution(mesh):
    in_specs = (
        P("dp", "seq", None),
        P("dp", "seq", None),
        P("dp", "seq", None),
        P(),
        P(),
        P(),
        P(),
        P(),
    )
    out_specs = (P("dp", None, "seq"), P(), P("seq", None), P(), P(), P())
    return jax.shard_map(
        per_device, mesh=mesh, in_specs=in_specs, out_specs=out_specs, check_vma=False
    )
```

profile of v0, /device:TPU:1, one launch (start us, length us, event | category | flops | bytes accessed | tf_op | source)
XLA Modules:
  0.0 925.9 jit_solution(2229353486682803280)
XLA Ops:
  11.0 64.1 %all-gather.6.cloned.1.call-done = bf16[1,4096,512]{2,1,0:T(8,128)(2,1)} async-done(((bf16[1,128,512]{2,1,0:T(8,128)(2,1)}), bf16[1,4096,512]{2,1,0:T(8,128)(2,1)}) %all-gather.6.cloned.1.call-update) | async-done | bytes 4194320 | tf_op jit(solution)/shard_map/all_gather | solution.py:107
  75.1 206.3 %while.32 = (s32[]{:T(128)}, f32[4,8,128]{2,1,0:T(8,128)S(1)}, f32[4,8,128]{2,1,0:T(8,128)S(1)}, s32[64]{0:T(128)S(1)}, s32[]{:T(128)}, /*index=5*/s32[128]{0:T(...) while((s32[]{:T(128)}, f32[4,8,128]{2,1,0:T(8,128)S(1)}, ...), condition=%wide.region_9.10_spmd, body=%wide.region_2.9_spmd.sunk | while | flops 68712320 | bytes 3713545 | solution.py:41
  83.4 1.7 conditional.4
  87.3 1.7 conditional.4
  156.9 1.7 conditional.4
  173.1 1.7 conditional.4
  184.9 1.7 conditional.4
  199.3 1.7 conditional.4
  221.6 1.7 conditional.4
  235.6 1.7 conditional.4
  239.5 1.7 conditional.4
  269.1 1.7 conditional.4
  281.5 212.6 %while.33 = (s32[]{:T(128)}, f32[4,4096]{1,0:T(4,128)S(1)}, s32[64]{0:T(128)S(1)}, s32[]{:T(128)}, s32[128]{0:T(128)S(1)}, /*index=5*/bf16[4096,512]{1,0:T(8,128...) while((s32[]{:T(128)}, f32[4,4096]{1,0:T(4,128)S(1)}, ...), condition=%wide.region_16.17_spmd, body=%wide.region_10.16_spmd.sunk | while | flops 68441992 | bytes 1416701 | solution.py:41
  494.1 2.0 copy.51
  496.2 4.8 multiply_convert_fusion
  501.0 164.5 %reduce-scatter.4.cloned.1.call-done = f32[128,4]{1,0:T(8,128)} async-done(((f32[4096,4]{1,0:T(8,128)}), f32[128,4]{1,0:T(8,128)}) %reduce-scatter.4.cloned.1.call-update) | async-done | bytes 2064
  668.3 2.5 copy.42
  670.8 63.7 %all_to_all.19 = bf16[128,32,256]{0,2,1:T(8,128)(2,1)S(1)} all-to-all(bf16[128,32,256]{0,2,1:T(8,128)(2,1)} %bitcast.50), channel_id=1, replica_groups=mesh['dp'=8,'seq'=32] {'seq'}, dimensions={1} | all-to-all | bytes 4194304 | tf_op jit(solution)/shard_map/all_to_all | solution.py:138
  734.5 2.9 copy.43
  737.4 19.9 %all-gather.4.cloned.1.call-done = bf16[4096,512]{1,0:T(8,128)(2,1)} async-done(((bf16[128,512]{1,0:T(8,128)(2,1)}), bf16[4096,512]{1,0:T(8,128)(2,1)}) %all-gather.4.cloned.1.call-update) | async-done | bytes 4194320 | tf_op jit(solution)/shard_map/all_gather | solution.py:139
  757.3 4.9 convolution_bitcast_fusion
  763.1 77.0 %all-reduce = (f32[]{:T(128)}, f32[4,512]{1,0:T(4,128)S(1)}, f32[512]{0:T(512)S(1)}, f32[4]{0:T(128)}) all-reduce(f32[]{:T(128)S(6)} %div.87, f32[4,512]{1,0:T(4,128)S(1)} %fusion.20, f32[512]{0:T(512)S(1)} %get-tuple-element.630, f32[4]{0:T(128)S(1)} %get-tuple-element.583), channel_id=1, replica_groups=mesh['dp'=8,'seq'=32] {'dp','seq'}, use_global_device_ids=true, to_apply=%region_19.20 | all-reduce | flops 2565 | bytes 20520 | tf_op jit(solution)/shard_map/psum | solution.py:143
  843.3 1.8 multiply_reduce_fusion
  845.7 70.9 %psum.44 = f32[]{:T(128)} all-reduce(f32[]{:T(128)} %multiply_reduce_fusion), channel_id=1, replica_groups=mesh['dp'=8,'seq'=32] {'seq'}, use_global_device_ids=true, to_apply=%region_22.23 | all-reduce | flops 1 | bytes 8 | tf_op jit(solution)/shard_map/psum | solution.py:147
  (1178 shorter events, 364.6 us)
Async XLA Ops:
  7.2 659.3 %copy-start = (bf16[4,512]{1,0:T(4,128)(2,1)S(1)}, bf16[4,512]{1,0:T(4,128)(2,1)}, u32[]{:S(2)}) copy-start(bf16[4,512]{1,0:T(4,128)(2,1)} %param.22) | copy-start | bytes 12292
  7.2 3.1 copy-start.4
  7.2 67.9 %all-gather.6.cloned.1.call-start = ((), (), s32[]{:S(2)}) async-start(), calls=%async_computation.4 | async-start | bytes 4325376 | tf_op jit(solution)/shard_map/all_gather | solution.py:107
  7.9 657.6 %reduce-scatter.4.cloned.1.call-start = ((), (), s32[]{:S(2)}) async-start(), calls=%async_computation.5 | async-start | bytes 2162688
  494.1 2.1 copy-start.1
  494.1 2.1 copy-start.2
  496.1 170.4 %copy-start.5 = (f32[4]{0:T(128)S(1)}, f32[4]{0:T(128)}, u32[]{:S(2)}) copy-start(f32[4]{0:T(128)} %param.23) | copy-start | bytes 52
  496.1 261.2 %all-gather.4.cloned.1.call-start = ((), (), s32[]{:S(2)}) async-start(), calls=%async_computation.2 | async-start | bytes 4325376 | tf_op jit(solution)/shard_map/all_gather | solution.py:139
  666.4 68.1 %copy-start.3 = (f32[4,128]{1,0:T(4,128)}, f32[4,128]{1,0:T(4,128)S(1)}, u32[]{:S(2)}) copy-start(f32[4,128]{1,0:T(4,128)S(1)} %copy.52) | copy-start | bytes 6148
  668.2 175.1 %all-reduce.3.cloned.1.call-start = ((), (), s32[]{:S(2)}) async-start(), calls=%async_computation.3 | async-start | bytes 1048576 | tf_op jit(solution)/shard_map/psum | solution.py:146
Sparse Core Ops, SparseCore 0:
  10.6 64.5 all-gather.5
  496.2 169.2 reduce-scatter.3
  668.7 88.6 all-gather.3
  762.4 72.5 all-reduce.2
where the time goes:
time: 935 us; the launch traced here: 926 us
  waiting for transfers between devices  249 us (27%)
  blocking collectives  212 us (23%)
  loops' own time  175 us (19%)
  other arithmetic  128 us (14%)
  local copies, waits for them, and re-layouts  92.1 us (10%)
  matrix products  52.9 us (6%)
  between operations  16.7 us (2%)
    another operation x2, loops' own time, blockwise(): return lax.fori_loop(0, rows_here // inner, visit_block, carried)  171 us
    unnamed x5, waiting for transfers between devices  165 us
    psum x1, blocking collectives, per_device(): lax.psum((second_part, first_bias_part, bias_part, loss_part), ('dp', 'se...  77 us
    psum x1, blocking collectives, per_device(): first_square = lax.psum(jnp.sum(first_grad * first_grad), 'seq')  70.9 us
    dynamic_slice x76, local copies, waits for them, and re-layouts, visit_block(): sub_rows = lax.dynamic_slice_in_dim(mass_portion, local_start, inner, 0)  64.7 us
    all_gather x1, waiting for transfers between devices, per_device(): keys_whole = lax.all_gather(local_key_rows, 'seq', axis=0, tiled=True)  64.1 us
    all_to_all x1, blocking collectives, per_device(): lax.all_to_all(tokens_in, 'seq', split_axis=1, concat_axis=0, tiled=True)  63.7 us
    reduce_min x64, other arithmetic, normalizer_step(): jnp.min(key_pos) > jnp.max(query_pos)  41.8 us
  transfers between devices with their start and end apart: 4, of which 3 were waited for; matrix products, arithmetic and copies ran while one was open for 2% of the time, Pallas kernels for 0%

commit v1 on v0

--- a/solution.py
+++ b/solution.py
@@ -104,7 +104,8 @@
         return normalizer_step(running, sub_rows, key_start, head_queries, query_pos, block_order)
 
     empty_mass = jnp.zeros((KEY_VALUE_HEADS, total_length), jnp.float32)
-    keys_whole = lax.all_gather(local_key_rows, "seq", axis=0, tiled=True)
+    sent = jnp.stack([local_key_rows] * lax.axis_size("seq"))
+    keys_whole = jnp.concatenate(lax.all_to_all(sent, "seq", 0, 0), axis=0)
     highest, summed = blockwise(keys_whole, 0, norm_update, start_state)
     log_total = highest + jnp.log(summed)
 

time: 935 us -> 980 us (1.048)
  waiting for transfers between devices: 249 us -> 279 us
  starting transfers between devices: 0.16 us -> 13.1 us
    all_to_all x0 -> x1, waiting for transfers between devices: none -> 91.1 us  [per_device(): keys_whole = jnp.concatenate(lax.all_to_all(sent, 'seq', 0, 0), axis=0)]
    all_gather x1 -> x0, waiting for transfers between devices: 64.1 us -> none  [per_device(): keys_whole = lax.all_gather(local_key_rows, 'seq', axis=0, tiled=True)]
    all_to_all x0 -> x1, starting transfers between devices: none -> 12.9 us  [per_device(): keys_whole = jnp.concatenate(lax.all_to_all(sent, 'seq', 0, 0), axis=0)]
    unnamed x5 -> x4, waiting for transfers between devices: 165 us -> 167 us
  transfers between devices with their start and end apart: 4 -> 4, of which waited for: 3 -> 3; matrix products, arithmetic and copies ran while one was open for 2% -> 1% of each run, Pallas kernels for 0% -> 0%
where the time goes in v1:
time: 980 us; the launch traced here: 971 us
  waiting for transfers between devices  279 us (28%)
  blocking collectives  212 us (22%)
  loops' own time  175 us (18%)
  other arithmetic  128 us (13%)
  local copies, waits for them, and re-layouts  94.4 us (10%)
  matrix products  53.1 us (5%)
  between operations  16.6 us (2%)
  starting transfers between devices  13.1 us (1%)
    another operation x2, loops' own time, blockwise(): return lax.fori_loop(0, rows_here // inner, visit_block, carried)  171 us
    unnamed x4, waiting for transfers between devices  167 us
    all_to_all x1, waiting for transfers between devices, per_device(): keys_whole = jnp.concatenate(lax.all_to_all(sent, 'seq', 0, 0), axis=0)  91.1 us
    psum x1, blocking collectives, per_device(): lax.psum((second_part, first_bias_part, bias_part, loss_part), ('dp', 'se...  77.2 us
    psum x1, blocking collectives, per_device(): first_square = lax.psum(jnp.sum(first_grad * first_grad), 'seq')  71 us
    dynamic_slice x76, local copies, waits for them, and re-layouts, visit_block(): sub_rows = lax.dynamic_slice_in_dim(mass_portion, local_start, inner, 0)  64.6 us
    all_to_all x1, blocking collectives, per_device(): lax.all_to_all(tokens_in, 'seq', split_axis=1, concat_axis=0, tiled=True)  63.8 us
    reduce_min x64, other arithmetic, mass_step(): jnp.min(key_pos) > jnp.max(query_pos)  41.8 us
  transfers between devices with their start and end apart: 4, of which 3 were waited for; matrix products, arithmetic and copies ran while one was open for 1% of the time, Pallas kernels for 0%

profile of v1, /device:TPU:1, one launch (start us, length us, event | category | flops | bytes accessed | tf_op | source)
XLA Modules:
  0.0 971.1 jit_solution(12285058296067650924)
XLA Ops:
  7.2 3.4 stack.3
  10.5 12.9 %all-to-all-start = ((bf16[32,128,512]{2,1,0:T(8,128)(2,1)}), bf16[32,128,512]{2,1,0:T(8,128)(2,1)}, u32[]{:S(2)}, u32[]{:S(2)}) async-start(bf16[32,128,512]{2,1,0:T(8,128)(2,1)} %stack.3), calls=%async_computation | async-start | bytes 8388608 | tf_op jit(solution)/shard_map/all_to_all | solution.py:108
  25.7 91.1 %all-to-all-done = bf16[32,128,512]{2,1,0:T(8,128)(2,1)} async-done(((bf16[32,128,512]{2,1,0:T(8,128)(2,1)}), bf16[32,128,512]{2,1,0:T(8,128)(2,1)}, u32[]{:S(2)}, u32[]{:S(2)}) %all-to-all-start) | async-done | bytes 4194336 | tf_op jit(solution)/shard_map/all_to_all | solution.py:108
  116.7 206.4 %while.32 = (s32[]{:T(128)}, f32[4,8,128]{2,1,0:T(8,128)S(1)}, f32[4,8,128]{2,1,0:T(8,128)S(1)}, s32[64]{0:T(128)S(1)}, s32[]{:T(128)}, /*index=5*/s32[128]{0:T(...) while((s32[]{:T(128)}, f32[4,8,128]{2,1,0:T(8,128)S(1)}, ...), condition=%wide.region_9.10_spmd, body=%wide.region_2.9_spmd.sunk | while | flops 68712320 | bytes 3713545 | solution.py:41
  121.1 1.7 conditional.4
  128.9 1.7 conditional.4
  160.1 1.7 conditional.4
  186.3 1.7 conditional.4
  194.7 1.7 conditional.4
  210.8 1.7 conditional.4
  234.9 1.7 conditional.4
  263.3 1.7 conditional.4
  323.2 212.7 %while.33 = (s32[]{:T(128)}, f32[4,4096]{1,0:T(4,128)S(1)}, s32[64]{0:T(128)S(1)}, s32[]{:T(128)}, s32[128]{0:T(128)S(1)}, /*index=5*/bf16[4096,512]{1,0:T(8,128...) while((s32[]{:T(128)}, f32[4,4096]{1,0:T(4,128)S(1)}, ...), condition=%wide.region_16.17_spmd, body=%wide.region_10.16_spmd.sunk | while | flops 68441992 | bytes 1416701 | solution.py:41
  535.9 2.0 copy.51
  538.0 4.8 multiply_convert_fusion
  542.8 166.6 %reduce-scatter.4.cloned.1.call-done = f32[128,4]{1,0:T(8,128)} async-done(((f32[4096,4]{1,0:T(8,128)}), f32[128,4]{1,0:T(8,128)}) %reduce-scatter.4.cloned.1.call-update) | async-done | bytes 2064
  712.1 2.5 copy.42
  714.6 63.8 %all_to_all.24 = bf16[128,32,256]{0,2,1:T(8,128)(2,1)S(1)} all-to-all(bf16[128,32,256]{0,2,1:T(8,128)(2,1)} %bitcast.51), channel_id=1, replica_groups=mesh['dp'=8,'seq'=32] {'seq'}, dimensions={1} | all-to-all | bytes 4194304 | tf_op jit(solution)/shard_map/all_to_all | solution.py:139
  778.4 2.9 copy.43
  781.3 21.0 %all-gather.2.cloned.1.call-done = bf16[4096,512]{1,0:T(8,128)(2,1)} async-done(((bf16[128,512]{1,0:T(8,128)(2,1)}), bf16[4096,512]{1,0:T(8,128)(2,1)}) %all-gather.2.cloned.1.call-update) | async-done | bytes 4194320 | tf_op jit(solution)/shard_map/all_gather | solution.py:140
  802.3 4.9 convolution_bitcast_fusion
  808.1 77.2 %all-reduce = (f32[]{:T(128)}, f32[4,512]{1,0:T(4,128)S(1)}, f32[512]{0:T(512)S(1)}, f32[4]{0:T(128)}) all-reduce(f32[]{:T(128)S(6)} %div.87, f32[4,512]{1,0:T(4,128)S(1)} %fusion.20, f32[512]{0:T(512)S(1)} %get-tuple-element.630, f32[4]{0:T(128)S(1)} %get-tuple-element.583), channel_id=1, replica_groups=mesh['dp'=8,'seq'=32] {'dp','seq'}, use_global_device_ids=true, to_apply=%region_19.20 | all-reduce | flops 2565 | bytes 20520 | tf_op jit(solution)/shard_map/psum | solution.py:144
  888.5 1.8 multiply_reduce_fusion
  890.8 71.0 %psum.44 = f32[]{:T(128)} all-reduce(f32[]{:T(128)} %multiply_reduce_fusion), channel_id=1, replica_groups=mesh['dp'=8,'seq'=32] {'seq'}, use_global_device_ids=true, to_apply=%region_22.23 | all-reduce | flops 1 | bytes 8 | tf_op jit(solution)/shard_map/psum | solution.py:148
  (1180 shorter events, 366.7 us)
Async XLA Ops:
  7.2 703.1 %copy-start = (bf16[4,512]{1,0:T(4,128)(2,1)S(1)}, bf16[4,512]{1,0:T(4,128)(2,1)}, u32[]{:S(2)}) copy-start(bf16[4,512]{1,0:T(4,128)(2,1)} %param.22) | copy-start | bytes 12292
  10.5 13.0 %copy-start.2 = (bf16[1,128,4096]{2,1,0:T(8,128)(2,1)S(1)}, bf16[1,128,4096]{2,1,0:T(8,128)(2,1)}, u32[]{:S(2)}) copy-start(bf16[1,128,4096]{2,1,0:T(8,128)(2,1)} %param.16) | copy-start | bytes 3145732
  10.5 106.2 %all-to-all-start = ((bf16[32,128,512]{2,1,0:T(8,128)(2,1)}), bf16[32,128,512]{2,1,0:T(8,128)(2,1)}, u32[]{:S(2)}, u32[]{:S(2)}) async-start(bf16[32,128,512]{2,1,0:T(8,128)(2,1)} %stack.3), calls=%async_computation | async-start | bytes 8388608 | tf_op jit(solution)/shard_map/all_to_all | solution.py:108
  23.5 1.4 copy-start.5
  23.5 685.9 %reduce-scatter.4.cloned.1.call-start = ((), (), s32[]{:S(2)}) async-start(), calls=%async_computation.5 | async-start | bytes 2162688
  535.9 2.1 copy-start.1
  535.9 2.1 copy-start.3
  537.9 172.4 %copy-start.6 = (f32[4]{0:T(128)S(1)}, f32[4]{0:T(128)}, u32[]{:S(2)}) copy-start(f32[4]{0:T(128)} %param.23) | copy-start | bytes 52
  537.9 264.4 %all-gather.2.cloned.1.call-start = ((), (), s32[]{:S(2)}) async-start(), calls=%async_computation.3 | async-start | bytes 4325376 | tf_op jit(solution)/shard_map/all_gather | solution.py:140
  710.3 68.1 %copy-start.4 = (f32[4,128]{1,0:T(4,128)}, f32[4,128]{1,0:T(4,128)S(1)}, u32[]{:S(2)}) copy-start(f32[4,128]{1,0:T(4,128)S(1)} %copy.52) | copy-start | bytes 6148
  712.1 176.4 %all-reduce.3.cloned.1.call-start = ((), (), s32[]{:S(2)}) async-start(), calls=%async_computation.4 | async-start | bytes 1048576 | tf_op jit(solution)/shard_map/psum | solution.py:147
Sparse Core Ops, SparseCore 0:
  538.0 171.3 reduce-scatter.3
  712.5 89.7 all-gather.1
  807.4 72.5 all-reduce.2
